TPU v7x, 32 devices: a whole 2x2x4 slice. The times are simulated.
32 devices in a mesh: group: 2 (over y), tm: 8 (over z, core), pix: 2 (over x), sub: 1.
Axes of the slice: x: 2, y: 2, z: 4, core: 2. Of those that a mesh axis runs over, the one named last changes fastest.
Arguments:
- anomaly: bfloat16 [512, 65536], P('tm', ('group', 'pix', 'sub')), parts along dimension 1, may hold values from -6 to 6
- offsets: int32 [32], replicated, may hold values from 0 to 256, as said below
- taper_index: int32 [32], replicated, may hold values from 0 to 3
Outputs:
- spectral_gram: float32 [256, 64, 64], P(('group', 'tm')), parts along dimension 0
- leading_energy: float32 [256], P(('group', 'tm')), parts along dimension 0
There are 2 independent parts, one for each index of `group`. A program takes and returns all parts, laid end to end along the dimension named above; an argument that names none is the same for every part. Nothing has to cross between parts.
Inputs may be any that keep to these rules, and one draw needn't show every extreme that they name: `offsets`: block starts never fall; the first block starts at day 0 and the last at day 512 - 256.
All inputs are finite; a program needn't handle non-finite values.
Results may differ from a plain program's by a relative error of at most 0.0034.
Values may be sent and summed in bfloat16 or wider, within the bound.
A program may use at most 128 MiB of HBM per device.

v0:
```python
import math
import jax
import jax.numpy as jnp
from jax import lax
from jax.sharding import PartitionSpec as P

NFFT = 256
NB = 32
POWER = 8
NF = 128
power_eps = 1e-06


def window_at(taper_index, steps_t, length):
    steps = steps_t.astype(jnp.float32)
    phase = steps * (2.0 * math.pi / length)
    center = (steps + 0.5) * (math.pi / length)
    hann = jnp.sin(center) ** 2
    hamming = 0.54 - 0.46 * jnp.cos(phase)
    blackman = 0.42 - 0.5 * jnp.cos(phase) + 0.08 * jnp.cos(2.0 * phase)
    sine_win = jnp.sin(center)
    which = taper_index[:, None]
    return jnp.where(
        which == 0, hann, jnp.where(which == 1, hamming, jnp.where(which == 2, blackman, sine_win))
    )


def day_operator(offsets, taper_index, freqs, days, length):
    day = jnp.arange(days, dtype=jnp.int32)
    step = day[None, :] - offsets[:, None]
    inside = (step >= 0) & (step < length)
    windows = jnp.where(inside, window_at(taper_index, step, length), 0.0)
    energy = 1.0 / jnp.sqrt(jnp.sum(windows * windows, axis=1, keepdims=True))
    scaled = windows * energy
    product = freqs[:, None, None] * step[None] & length - 1
    angle = product.astype(jnp.float32) * (2.0 * math.pi / length)
    table = jnp.stack([jnp.cos(angle), -jnp.sin(angle)], axis=1)
    table = lax.reduce_precision(table, 8, 7)
    return (table * scaled).reshape(freqs.shape[0], 2 * offsets.shape[0], days)


def shards(anomaly, offsets, taper_index):
    series = lax.all_to_all(anomaly, "tm", split_axis=1, concat_axis=0, tiled=True)
    days = series.shape[0]
    own = NF // lax.axis_size("tm")
    freqs = lax.axis_index("tm") * own + jnp.arange(own, dtype=jnp.int32)
    operator = day_operator(offsets, taper_index, freqs, days, NFFT)
    covariance = jnp.einsum("dp,ep->de", series, series, preferred_element_type=jnp.float32)
    covariance = lax.psum(covariance, ("tm", "pix", "sub"))
    total_pixels = anomaly.shape[1] * lax.axis_size(("pix", "sub"))
    half = jnp.einsum("fid,de->fie", operator, covariance, precision=lax.Precision.HIGH)
    spectral_gram = jnp.einsum("fie,fje->fij", half, operator, precision=lax.Precision.HIGH)
    spectral_gram = spectral_gram / total_pixels
    vector = jnp.ones((own, 2 * NB), jnp.float32)
    for _ in range(POWER):
        applied = jnp.einsum("fij,fj->fi", spectral_gram, vector, precision=lax.Precision.HIGHEST)
        vector = applied / jnp.sqrt(jnp.mean(applied * applied, axis=1, keepdims=True) + power_eps)
    applied = jnp.einsum("fij,fj->fi", spectral_gram, vector, precision=lax.Precision.HIGHEST)
    leading_energy = jnp.sqrt(jnp.mean(applied * applied, axis=1))
    return (spectral_gram, leading_energy)


def solution(mesh):
    placed = (P("tm", ("group", "pix", "sub")), P(), P())
    return jax.shard_map(
        shards,
        mesh=mesh,
        in_specs=placed,
        out_specs=(P(("group", "tm"), None, None), P(("group", "tm"))),
        check_vma=False,
    )
```

profile of v0, /device:TPU:0, one launch (start us, length us, event | category | flops | bytes accessed | tf_op | source)
XLA Modules:
  0.0 184.7 jit_solution(9127771249241529888)
XLA Ops:
  7.2 3.1 %copy.28 = bf16[8,8,8,2048]{3,2,0,1:T(8,128)(2,1)} copy(bf16[8,8,8,2048]{3,2,1,0:T(8,128)(2,1)} %bitcast.79) | data formatting | bytes 4194304 | tf_op jit(solution)/shard_map/all_to_all | solution.py:43
  10.3 0.0 copy-start.2
  10.3 0.0 copy-start.1
  10.3 6.5 %all-to-all-start = ((bf16[64,8,2048]{2,0,1:T(8,128)(2,1)}), bf16[64,8,2048]{2,0,1:T(8,128)(2,1)}, u32[]{:S(2)}, u32[]{:S(2)}) async-start(bf16[64,8,2048]{2,0,1:T(8,128)(2,1)} %bitcast.78), calls=%async_computation | async-start | bytes 4194304 | tf_op jit(solution)/shard_map/all_to_all | solution.py:43
  16.8 0.0 all-reduce.2.cloned.1.call-start
  16.8 0.0 copy-done.2
  16.8 0.0 copy-done.1
  16.8 0.9 multiply_reduce_fusion
  17.7 0.1 iota_subtract_fusion
  17.8 3.8 %fusion.2 = (f32[16,1,32,512]{3,2,1,0:T(8,128)S(1)}, f32[16,1,32,512]{3,2,1,0:T(8,128)S(1)}) fusion(s32[32,512]{1,0:T(8,128)S(1)} %iota_subtract_fusion, s32[16]{0:T(128)S(1)} %iota_add_fusion), kind=kLoop, calls=%fused_computation.8 | loop fusion | flops 1310720 | bytes 2162752 | tf_op jit(solution)/shard_map/cos | solution.py:37
  21.6 44.3 %all-to-all-done = bf16[64,8,2048]{2,0,1:T(8,128)(2,1)} async-done(((bf16[64,8,2048]{2,0,1:T(8,128)(2,1)}), bf16[64,8,2048]{2,0,1:T(8,128)(2,1)}, u32[]{:S(2)}, u32[]{:S(2)}) %all-to-all-start) | async-done | bytes 2097184 | tf_op jit(solution)/shard_map/all_to_all | solution.py:43
  65.9 4.5 %fusion.6 = f32[512,512]{1,0:T(8,128)} fusion(bf16[512,2048]{1,0:T(8,128)(2,1)} %bitcast.3), kind=kOutput, calls=%fused_computation.46 | convolution fusion | flops 1073741824 | bytes 3145728 | tf_op jit(solution)/shard_map/dp,ep->de/dot_general | solution.py:48
  70.4 0.0 all-reduce.2.cloned.1.call-update
  70.4 0.8 broadcast_multiply_fusion
  71.2 0.2 maximum_reduce-precision_fusion
  71.5 0.3 bitcast_multiply_fusion
  71.8 90.9 %all-reduce.2.cloned.1.call-done = f32[512,512]{1,0:T(8,128)} async-done(((f32[512,512]{1,0:T(8,128)}), f32[512,512]{1,0:T(8,128)}) %all-reduce.2.cloned.1.call-update) | async-done | bytes 1048592 | tf_op jit(solution)/shard_map/psum | solution.py:49
  162.7 3.0 %fusion = f32[16,64,512]{2,1,0:T(8,128)S(1)} fusion(f32[16,64,512]{2,1,0:T(8,128)S(1)} %bitcast_multiply_fusion, f32[512,512]{1,0:T(8,128)} %all-reduce.2.cloned.1.call-done), kind=kOutput, calls=%fused_computation.4 | convolution fusion | flops 1610612736 | bytes 5242880 | tf_op jit(solution)/shard_map/fid,de->fie/dot_general | solution.py:51
  165.7 1.1 convolution_multiply_fusion
  166.8 0.0 copy-start
  166.9 0.9 fusion.7
  167.8 0.1 multiply_reduce_fusion.9
  167.9 0.1 broadcast_divide_fusion.7
  168.0 0.9 fusion.8
  168.9 0.1 multiply_reduce_fusion.8
  169.1 0.1 broadcast_divide_fusion.6
  169.2 0.9 fusion.9
  170.1 0.1 multiply_reduce_fusion.7
  170.2 0.1 broadcast_divide_fusion.5
  170.3 1.1 fusion.10
  171.4 0.1 multiply_reduce_fusion.6
  171.6 0.1 broadcast_divide_fusion.4
  171.6 0.9 fusion.11
  172.6 0.1 multiply_reduce_fusion.5
  172.7 0.1 broadcast_divide_fusion.3
  172.8 0.9 fusion.12
  173.7 0.1 multiply_reduce_fusion.4
  173.9 0.1 broadcast_divide_fusion.2
  173.9 0.9 fusion.13
  174.9 0.1 multiply_reduce_fusion.3
  175.0 0.1 broadcast_divide_fusion.1
  175.1 0.9 fusion.14
  176.0 0.1 multiply_reduce_fusion.2
  176.2 0.1 broadcast_divide_fusion
  176.2 0.0 copy-done
  176.2 0.9 fusion.15
  177.2 0.1 multiply_reduce_fusion.1
  177.3 0.5 multiply_sqrt_fusion
  (13 shorter events, 0.1 us)
Async XLA Ops:
  10.3 6.5 %copy-start.2 = (s32[32]{0:T(128)S(1)}, s32[32]{0:T(128)}, u32[]{:S(2)}) copy-start(s32[32]{0:T(128)} %param.5) | copy-start | bytes 388
  10.3 6.5 %copy-start.1 = (s32[32]{0:T(128)S(1)}, s32[32]{0:T(128)}, u32[]{:S(2)}) copy-start(s32[32]{0:T(128)} %param.4) | copy-start | bytes 388
  10.3 55.6 %all-to-all-start = ((bf16[64,8,2048]{2,0,1:T(8,128)(2,1)}), bf16[64,8,2048]{2,0,1:T(8,128)(2,1)}, u32[]{:S(2)}, u32[]{:S(2)}) async-start(bf16[64,8,2048]{2,0,1:T(8,128)(2,1)} %bitcast.78), calls=%async_computation | async-start | bytes 4194304 | tf_op jit(solution)/shard_map/all_to_all | solution.py:43
  16.8 145.9 %all-reduce.2.cloned.1.call-start = ((), (), s32[]{:S(2)}) async-start(), calls=%async_computation.1 | async-start | bytes 2097152 | tf_op jit(solution)/shard_map/psum | solution.py:49
  166.8 9.4 %copy-start = (f32[16,64,64]{2,1,0:T(8,128)}, f32[16,64,64]{2,1,0:T(8,128)S(1)}, u32[]{:S(2)}) copy-start(f32[16,64,64]{2,1,0:T(8,128)S(1)} %convolution_multiply_fusion) | copy-start | bytes 786436
Sparse Core Ops, SparseCore 0:
  70.6 92.0 all-reduce.1
where the time goes:
time: 185 us
  waiting for transfers between devices  135 us (73%)
  matrix products  17.3 us (9%)
  between operations  14.2 us (8%)
  other arithmetic  8.3 us (4%)
  starting transfers between devices  6.49 us (4%)
  local copies, waits for them, and re-layouts  3.17 us (2%)
    psum x1, waiting for transfers between devices, shards(): covariance = lax.psum(covariance, ('tm', 'pix', 'sub'))  90.9 us
    all_to_all x1, waiting for transfers between devices, shards(): lax.all_to_all(anomaly, 'tm', split_axis=1, concat_axis=0, tiled=True)  44.3 us
    dot_general x9, matrix products, shards(): jnp.einsum('fij,fj->fi', spectral_gram, vector, precision=lax.Precision.H...  8.59 us
    all_to_all x1, starting transfers between devices, shards(): lax.all_to_all(anomaly, 'tm', split_axis=1, concat_axis=0, tiled=True)  6.46 us
    dot_general x1, matrix products, shards(): jnp.einsum('dp,ep->de', series, series, preferred_element_type=jnp.float32)  4.49 us
    cos x1, other arithmetic, day_operator(): table = jnp.stack([jnp.cos(angle), -jnp.sin(angle)], axis=1)  3.82 us
  transfers between devices with their start and end apart: 2, of which 2 were waited for; matrix products, arithmetic and copies ran while one was open for 3% of the time, Pallas kernels for 0%

commit v1 on v0

--- a/solution.py
+++ b/solution.py
@@ -46,7 +46,7 @@
     freqs = lax.axis_index("tm") * own + jnp.arange(own, dtype=jnp.int32)
     operator = day_operator(offsets, taper_index, freqs, days, NFFT)
     covariance = jnp.einsum("dp,ep->de", series, series, preferred_element_type=jnp.float32)
-    covariance = lax.psum(covariance, ("tm", "pix", "sub"))
+    covariance = lax.psum(lax.psum(covariance, ("pix", "sub")), "tm")
     total_pixels = anomaly.shape[1] * lax.axis_size(("pix", "sub"))
     half = jnp.einsum("fid,de->fie", operator, covariance, precision=lax.Precision.HIGH)
     spectral_gram = jnp.einsum("fie,fje->fij", half, operator, precision=lax.Precision.HIGH)

time: 185 us -> 189 us (1.022)
  blocking collectives: 0 us -> 55.2 us
  waiting for transfers between devices: 135 us -> 94.2 us
  starting transfers between devices: 6.49 us -> 0.08 us
  matrix products: 17.3 us -> 14.9 us
    all_to_all x0 -> x1, blocking collectives: none -> 55.2 us  [shards(): lax.all_to_all(anomaly, 'tm', split_axis=1, concat_axis=0, tiled=True)]
    all_to_all x1 -> x0, waiting for transfers between devices: 44.3 us -> none  [shards(): lax.all_to_all(anomaly, 'tm', split_axis=1, concat_axis=0, tiled=True)]
    all_to_all x1 -> x0, starting transfers between devices: 6.46 us -> none  [shards(): lax.all_to_all(anomaly, 'tm', split_axis=1, concat_axis=0, tiled=True)]
    psum x1 -> x2, waiting for transfers between devices: 90.9 us -> 94.2 us  [shards(): covariance = lax.psum(lax.psum(covariance, ('pix', 'sub')), 'tm')]
    dot_general x1, matrix products: 4.49 us -> 2.32 us  [shards(): jnp.einsum('dp,ep->de', series, series, preferred_element_type=jnp.float32)]
where the time goes in v1:
time: 189 us
  waiting for transfers between devices  94.2 us (50%)
  blocking collectives  55.2 us (29%)
  matrix products  14.9 us (8%)
  between operations  14.3 us (8%)
  other arithmetic  8.3 us (4%)
    psum x2, waiting for transfers between devices, shards(): covariance = lax.psum(lax.psum(covariance, ('pix', 'sub')), 'tm')  94.2 us
    all_to_all x1, blocking collectives, shards(): lax.all_to_all(anomaly, 'tm', split_axis=1, concat_axis=0, tiled=True)  55.2 us
    dot_general x9, matrix products, shards(): jnp.einsum('fij,fj->fi', spectral_gram, vector, precision=lax.Precision.H...  8.43 us
    cos x1, other arithmetic, day_operator(): table = jnp.stack([jnp.cos(angle), -jnp.sin(angle)], axis=1)  3.82 us
  transfers between devices with their start and end apart: 2, of which 2 were waited for; matrix products, arithmetic and copies ran while one was open for 3% of the time, Pallas kernels for 0%

profile of v1, /device:TPU:0, one launch (start us, length us, event | category | flops | bytes accessed | tf_op | source)
XLA Modules:
  0.0 188.7 jit_solution(14603781749783120951)
XLA Ops:
  7.2 0.0 all-reduce.3.cloned.1.call-start
  7.2 1.7 copy.28
  8.9 55.2 %all_to_all.19 = bf16[64,8,2048]{2,0,1:T(8,128)(2,1)S(1)} all-to-all(bf16[64,8,2048]{2,0,1:T(8,128)(2,1)S(1)} %bitcast.79), channel_id=1, replica_groups=mesh['group'=2,'tm'=8,'pix'=2,'sub'=1] {'tm'}, dimensions={1} | all-to-all | bytes 4194304 | tf_op jit(solution)/shard_map/all_to_all | solution.py:43
  64.1 0.0 copy-start.2
  64.1 0.0 copy-start.1
  64.1 2.3 %fusion.6 = f32[512,512]{1,0:T(8,128)} fusion(bf16[512,2048]{1,0:T(8,128)(2,1)S(1)} %bitcast.81), kind=kOutput, calls=%fused_computation.46 | convolution fusion | flops 1073741824 | bytes 3145728 | tf_op jit(solution)/shard_map/dp,ep->de/dot_general | solution.py:48
  66.5 0.0 all-reduce.3.cloned.1.call-update
  66.5 0.0 all-reduce.5.cloned.1.call-start
  66.5 0.0 copy-done.2
  66.6 0.0 copy-done.1
  66.6 0.9 multiply_reduce_fusion
  67.4 0.1 iota_subtract_fusion
  67.5 3.8 %fusion.2 = (f32[16,1,32,512]{3,2,1,0:T(8,128)S(1)}, f32[16,1,32,512]{3,2,1,0:T(8,128)S(1)}) fusion(s32[32,512]{1,0:T(8,128)S(1)} %iota_subtract_fusion, s32[16]{0:T(128)S(1)} %iota_add_fusion), kind=kLoop, calls=%fused_computation.8 | loop fusion | flops 1310720 | bytes 2162752 | tf_op jit(solution)/shard_map/cos | solution.py:37
  71.4 34.2 %all-reduce.3.cloned.1.call-done = f32[512,512]{1,0:T(8,128)} async-done(((f32[512,512]{1,0:T(8,128)}), f32[512,512]{1,0:T(8,128)}) %all-reduce.3.cloned.1.call-update) | async-done | bytes 1048592 | tf_op jit(solution)/shard_map/psum | solution.py:49
  105.6 0.0 all-reduce.5.cloned.1.call-update
  105.6 0.8 broadcast_multiply_fusion
  106.4 0.2 maximum_reduce-precision_fusion
  106.6 0.3 bitcast_multiply_fusion
  106.9 60.0 %all-reduce.5.cloned.1.call-done = f32[512,512]{1,0:T(8,128)} async-done(((f32[512,512]{1,0:T(8,128)}), f32[512,512]{1,0:T(8,128)}) %all-reduce.5.cloned.1.call-update) | async-done | bytes 1048592 | tf_op jit(solution)/shard_map/psum | solution.py:49
  166.9 3.1 %fusion = f32[16,64,512]{2,1,0:T(8,128)S(1)} fusion(f32[16,64,512]{2,1,0:T(8,128)S(1)} %bitcast_multiply_fusion, f32[512,512]{1,0:T(8,128)} %all-reduce.5.cloned.1.call-done), kind=kOutput, calls=%fused_computation.4 | convolution fusion | flops 1610612736 | bytes 5242880 | tf_op jit(solution)/shard_map/fid,de->fie/dot_general | solution.py:51
  170.0 1.1 convolution_multiply_fusion
  171.1 0.0 copy-start
  171.1 0.9 fusion.7
  172.0 0.1 multiply_reduce_fusion.9
  172.2 0.1 broadcast_divide_fusion.7
  172.2 0.9 fusion.8
  173.2 0.1 multiply_reduce_fusion.8
  173.3 0.1 broadcast_divide_fusion.6
  173.4 0.9 fusion.9
  174.3 0.1 multiply_reduce_fusion.7
  174.5 0.1 broadcast_divide_fusion.5
  174.5 0.9 fusion.10
  175.5 0.1 multiply_reduce_fusion.6
  175.6 0.1 broadcast_divide_fusion.4
  175.7 0.9 fusion.11
  176.6 0.1 multiply_reduce_fusion.5
  176.8 0.1 broadcast_divide_fusion.3
  176.8 0.9 fusion.12
  177.8 0.1 multiply_reduce_fusion.4
  177.9 0.1 broadcast_divide_fusion.2
  178.0 0.9 fusion.13
  178.9 0.1 multiply_reduce_fusion.3
  179.1 0.1 broadcast_divide_fusion.1
  179.1 0.9 fusion.14
  180.1 0.1 multiply_reduce_fusion.2
  180.2 0.1 broadcast_divide_fusion
  180.3 0.0 copy-done
  180.3 0.9 fusion.15
  181.2 0.1 multiply_reduce_fusion.1
  181.4 0.5 multiply_sqrt_fusion
  (13 shorter events, 0.1 us)
Async XLA Ops:
  7.2 98.4 %all-reduce.3.cloned.1.call-start = ((), (), s32[]{:S(2)}) async-start(), calls=%async_computation.1 | async-start | bytes 2097152 | tf_op jit(solution)/shard_map/psum | solution.py:49
  64.1 2.4 %copy-start.2 = (s32[32]{0:T(128)S(1)}, s32[32]{0:T(128)}, u32[]{:S(2)}) copy-start(s32[32]{0:T(128)} %param.5) | copy-start | bytes 388
  64.1 2.4 %copy-start.1 = (s32[32]{0:T(128)S(1)}, s32[32]{0:T(128)}, u32[]{:S(2)}) copy-start(s32[32]{0:T(128)} %param.4) | copy-start | bytes 388
  66.5 100.4 %all-reduce.5.cloned.1.call-start = ((), (), s32[]{:S(2)}) async-start(), calls=%async_computation.2 | async-start | bytes 2097152 | tf_op jit(solution)/shard_map/psum | solution.py:49
  171.1 9.2 %copy-start = (f32[16,64,64]{2,1,0:T(8,128)}, f32[16,64,64]{2,1,0:T(8,128)S(1)}, u32[]{:S(2)}) copy-start(f32[16,64,64]{2,1,0:T(8,128)S(1)} %convolution_multiply_fusion) | copy-start | bytes 786436
Sparse Core Ops, SparseCore 0:
  66.6 38.9 all-reduce.2
  108.1 58.7 all-reduce.4

commit v2 on v0

--- a/solution.py
+++ b/solution.py
@@ -46,7 +46,7 @@
     freqs = lax.axis_index("tm") * own + jnp.arange(own, dtype=jnp.int32)
     operator = day_operator(offsets, taper_index, freqs, days, NFFT)
     covariance = jnp.einsum("dp,ep->de", series, series, preferred_element_type=jnp.float32)
-    covariance = lax.psum(covariance, ("tm", "pix", "sub"))
+    covariance = jnp.sum(lax.all_gather(covariance, ("tm", "pix", "sub")), axis=0)
     total_pixels = anomaly.shape[1] * lax.axis_size(("pix", "sub"))
     half = jnp.einsum("fid,de->fie", operator, covariance, precision=lax.Precision.HIGH)
     spectral_gram = jnp.einsum("fie,fje->fij", half, operator, precision=lax.Precision.HIGH)

time: 185 us -> 221 us (1.19)
  blocking collectives: 0 us -> 55.2 us
  waiting for transfers between devices: 135 us -> 120 us
  other arithmetic: 8.3 us -> 16.3 us
  starting transfers between devices: 6.49 us -> 0.04 us
  matrix products: 17.3 us -> 13.8 us
    all_gather x0 -> x1, waiting for transfers between devices: none -> 120 us  [shards(): lax.all_gather(covariance, ('tm', 'pix', 'sub'))]
    psum x1 -> x0, waiting for transfers between devices: 90.9 us -> none  [shards(): covariance = lax.psum(covariance, ('tm', 'pix', 'sub'))]
    all_to_all x0 -> x1, blocking collectives: none -> 55.2 us  [shards(): lax.all_to_all(anomaly, 'tm', split_axis=1, concat_axis=0, tiled=True)]
    all_to_all x1 -> x0, waiting for transfers between devices: 44.3 us -> none  [shards(): lax.all_to_all(anomaly, 'tm', split_axis=1, concat_axis=0, tiled=True)]
    reduce_sum x0 -> x1, other arithmetic: none -> 7.91 us  [shards(): jnp.sum(lax.all_gather(covariance, ('tm', 'pix', 'sub')), axis=0)]
    all_to_all x1 -> x0, starting transfers between devices: 6.46 us -> none  [shards(): lax.all_to_all(anomaly, 'tm', split_axis=1, concat_axis=0, tiled=True)]
    dot_general x1, matrix products: 4.49 us -> 2.27 us  [shards(): jnp.einsum('dp,ep->de', series, series, preferred_element_type=jnp.float32)]
  transfers between devices with their start and end apart: 2 -> 1, of which waited for: 2 -> 1; matrix products, arithmetic and copies ran while one was open for 3% -> 3% of each run, Pallas kernels for 0% -> 0%
where the time goes in v2:
time: 221 us
  waiting for transfers between devices  120 us (54%)
  blocking collectives  55.2 us (25%)
  other arithmetic  16.3 us (7%)
  between operations  14.2 us (6%)
  matrix products  13.8 us (6%)
    all_gather x1, waiting for transfers between devices, shards(): lax.all_gather(covariance, ('tm', 'pix', 'sub'))  120 us
    all_to_all x1, blocking collectives, shards(): lax.all_to_all(anomaly, 'tm', split_axis=1, concat_axis=0, tiled=True)  55.2 us
    dot_general x9, matrix products, shards(): jnp.einsum('fij,fj->fi', spectral_gram, vector, precision=lax.Precision.H...  8.61 us
    reduce_sum x1, other arithmetic, shards(): jnp.sum(lax.all_gather(covariance, ('tm', 'pix', 'sub')), axis=0)  7.91 us
  transfers between devices with their start and end apart: 1, of which 1 were waited for; matrix products, arithmetic and copies ran while one was open for 3% of the time, Pallas kernels for 0%

profile of v2, /device:TPU:0, one launch (start us, length us, event | category | flops | bytes accessed | tf_op | source)
XLA Modules:
  0.0 221.0 jit_solution(10445171916750966675)
XLA Ops:
  7.2 0.0 all-gather.3.cloned.1.call-start
  7.2 1.7 copy.28
  8.9 55.2 %all_to_all.19 = bf16[64,8,2048]{2,0,1:T(8,128)(2,1)S(1)} all-to-all(bf16[64,8,2048]{2,0,1:T(8,128)(2,1)S(1)} %bitcast.81), channel_id=1, replica_groups=mesh['group'=2,'tm'=8,'pix'=2,'sub'=1] {'tm'}, dimensions={1} | all-to-all | bytes 4194304 | tf_op jit(solution)/shard_map/all_to_all | solution.py:43
  64.1 0.0 copy-start.2
  64.1 0.0 copy-start.1
  64.1 2.3 %fusion.6 = f32[512,512]{1,0:T(8,128)} fusion(bf16[512,2048]{1,0:T(8,128)(2,1)S(1)} %bitcast.83), kind=kOutput, calls=%fused_computation.46 | convolution fusion | flops 1073741824 | bytes 3145728 | tf_op jit(solution)/shard_map/dp,ep->de/dot_general | solution.py:48
  66.4 0.0 all-gather.3.cloned.1.call-update
  66.4 0.0 copy-done.2
  66.5 0.0 copy-done.1
  66.5 0.9 multiply_reduce_fusion
  67.4 0.1 iota_subtract_fusion
  67.4 3.8 %fusion.2 = (f32[16,1,32,512]{3,2,1,0:T(8,128)S(1)}, f32[16,1,32,512]{3,2,1,0:T(8,128)S(1)}) fusion(s32[32,512]{1,0:T(8,128)S(1)} %iota_subtract_fusion, s32[16]{0:T(128)S(1)} %iota_add_fusion), kind=kLoop, calls=%fused_computation.8 | loop fusion | flops 1310720 | bytes 2162752 | tf_op jit(solution)/shard_map/cos | solution.py:37
  71.3 0.3 maximum_reduce-precision_fusion
  71.6 0.8 broadcast_multiply_fusion
  72.4 0.3 bitcast_multiply_fusion
  72.7 119.6 %all-gather.3.cloned.1.call-done = f32[8192,512]{1,0:T(8,128)} async-done(((f32[512,512]{1,0:T(8,128)}), f32[8192,512]{1,0:T(8,128)}) %all-gather.3.cloned.1.call-update) | async-done | bytes 16777232 | tf_op jit(solution)/shard_map/all_gather | solution.py:49
  192.3 7.9 %reduce_sum.100 = f32[512,512]{1,0:T(8,128)S(1)} reduce(f32[16,512,512]{2,1,0:T(8,128)} %bitcast.80, f32[]{:T(128)} %constant.54.clone.1), dimensions={0}, to_apply=%region_1.2 | reduce | flops 3932160 | bytes 17825796 | tf_op jit(solution)/shard_map/reduce_sum | solution.py:49
  200.2 1.8 fusion
  202.0 1.1 convolution_multiply_fusion
  203.2 0.0 copy-start
  203.2 1.1 fusion.7
  204.3 0.1 multiply_reduce_fusion.9
  204.4 0.1 broadcast_divide_fusion.7
  204.5 0.9 fusion.8
  205.5 0.1 multiply_reduce_fusion.8
  205.6 0.1 broadcast_divide_fusion.6
  205.7 0.9 fusion.9
  206.6 0.1 multiply_reduce_fusion.7
  206.7 0.1 broadcast_divide_fusion.5
  206.8 0.9 fusion.10
  207.8 0.1 multiply_reduce_fusion.6
  207.9 0.1 broadcast_divide_fusion.4
  208.0 0.9 fusion.11
  208.9 0.1 multiply_reduce_fusion.5
  209.0 0.1 broadcast_divide_fusion.3
  209.1 0.9 fusion.12
  210.1 0.1 multiply_reduce_fusion.4
  210.2 0.1 broadcast_divide_fusion.2
  210.3 0.9 fusion.13
  211.2 0.1 multiply_reduce_fusion.3
  211.4 0.1 broadcast_divide_fusion.1
  211.4 0.9 fusion.14
  212.4 0.1 multiply_reduce_fusion.2
  212.5 0.1 broadcast_divide_fusion
  212.6 0.0 copy-done
  212.6 0.9 fusion.15
  213.5 0.1 multiply_reduce_fusion.1
  213.6 0.5 multiply_sqrt_fusion
  (13 shorter events, 0.1 us)
Async XLA Ops:
  7.2 185.1 %all-gather.3.cloned.1.call-start = ((), (), s32[]{:S(2)}) async-start(), calls=%async_computation.1 | async-start | bytes 17825792 | tf_op jit(solution)/shard_map/all_gather | solution.py:49
  64.1 2.3 %copy-start.2 = (s32[32]{0:T(128)S(1)}, s32[32]{0:T(128)}, u32[]{:S(2)}) copy-start(s32[32]{0:T(128)} %param.5) | copy-start | bytes 388
  64.1 2.3 %copy-start.1 = (s32[32]{0:T(128)S(1)}, s32[32]{0:T(128)}, u32[]{:S(2)}) copy-start(s32[32]{0:T(128)} %param.4) | copy-start | bytes 388
  203.2 9.4 %copy-start = (f32[16,64,64]{2,1,0:T(8,128)}, f32[16,64,64]{2,1,0:T(8,128)S(1)}, u32[]{:S(2)}) copy-start(f32[16,64,64]{2,1,0:T(8,128)S(1)} %convolution_multiply_fusion) | copy-start | bytes 786436
Sparse Core Ops, SparseCore 0:
  66.6 125.6 all-gather.2
